TPU v7x, 32 devices: a whole 2x2x4 slice. The times are simulated.
32 devices in a mesh: dp: 16 (over z, y, x), mp: 2 (over core).
Axes of the slice: x: 2, y: 2, z: 4, core: 2. Of those that a mesh axis runs over, the one named last changes fastest.
Arguments:
- residual: bfloat16 [256, 4608], P(None, 'dp'), may hold values from -60 to 60
- norm_gain: float32 [4608], P('dp'), may hold values from 0.25 to 1.75
- query_weight: bfloat16 [4608, 2048], P('dp', 'mp'), may hold values from -2 to 2
- key_weight: bfloat16 [4608, 1024], P('dp', 'mp'), may hold values from -2 to 2
- value_weight: bfloat16 [4608, 1024], P('dp', 'mp'), may hold values from -0.09375 to 0.09375
- out_weight: bfloat16 [2048, 4608], P('mp', 'dp'), may hold values from -1 to 1
- post_gain: float32 [4608], P('dp'), may hold values from 0.25 to 1.75
- encoder_weight: bfloat16 [4608, 8192], P(None, ('dp', 'mp')), may hold values from -0.09375 to 0.09375
- encoder_bias: float32 [8192], P(('dp', 'mp')), may hold values from -3 to 3
- decoder_weight: bfloat16 [8192, 4608], P(('dp', 'mp')), may hold values from -0.125 to 0.125
- decoder_bias: float32 [4608], replicated, may hold values from -3 to 3
Outputs:
- encoder_grad: bfloat16 [4608, 8192], P(None, ('dp', 'mp'))
- encoder_bias_grad: float32 [8192], P(('dp', 'mp'))
- decoder_grad: bfloat16 [8192, 4608], P(('dp', 'mp'))
All inputs are finite; a program needn't handle non-finite values.
Results may differ from a plain program's by a relative error of at most 0.015.
Values may be sent and summed in bfloat16 or wider, within the bound.
No kernel may reach another device: no remote copies, remote signals or barrier semaphores. Data moves between devices by JAX's collectives and lax.ppermute only.
A program may use at most 128 MiB of HBM per device.

v0:
```python
import jax
import jax.numpy as jnp
from jax import lax
from jax.sharding import PartitionSpec as P

HEAD_DIM = 128
epsilon = 1e-06
softcap = 50.0
query_scale = 1.0 / 12.0
rope_base = 10000.0
smoothing = 0.1
penalty = 1.0
loss_weight = 0.0625


def rotate(matrix, positions):
    half_dim = matrix.shape[-1] // 2
    frequency = rope_base ** (-2.0 * jnp.arange(half_dim, dtype=jnp.float32) / matrix.shape[-1])
    angles = positions.astype(jnp.float32)[:, None] * frequency[None, :]
    cosine = jnp.cos(angles)[:, None, :]
    sine_part = jnp.sin(angles)[:, None, :]
    front_half = matrix[..., :half_dim]
    back_half = matrix[..., half_dim:]
    return jnp.concatenate(
        [front_half * cosine - back_half * sine_part, back_half * cosine + front_half * sine_part],
        axis=-1,
    )


def project(summed, square_sum, positions, model_width, query_width, key_width, head_dim):
    inverse = lax.rsqrt(square_sum / model_width + epsilon)
    scaled = summed * inverse[:, None]
    row_count = scaled.shape[0]
    queries = rotate(scaled[:, :query_width].reshape(row_count, -1, head_dim), positions).astype(
        jnp.bfloat16
    )
    keys = rotate(
        scaled[:, query_width : query_width + key_width].reshape(row_count, -1, head_dim), positions
    ).astype(jnp.bfloat16)
    values = (
        scaled[:, query_width + key_width :].reshape(row_count, -1, head_dim).astype(jnp.bfloat16)
    )
    return (queries, keys, values)


def partial_attention(queries, keys, values, query_positions, key_positions):
    row_count, query_heads, head_dim = queries.shape
    key_heads = keys.shape[1]
    grouped = queries.reshape(row_count, key_heads, query_heads // key_heads, head_dim)
    scores = (
        jnp.einsum("rkgd,skd->kgrs", grouped, keys, preferred_element_type=jnp.float32)
        * query_scale
    )
    capped = softcap * jnp.tanh(scores / softcap)
    allowed = query_positions[:, None] >= key_positions[None, :]
    weights = jnp.where(allowed, jnp.exp(capped), 0.0)
    denominator = jnp.sum(weights, axis=3)
    numerator = jnp.einsum(
        "kgrs,skd->rkgd", weights.astype(jnp.bfloat16), values, preferred_element_type=jnp.float32
    )
    return (
        numerator.reshape(row_count, query_heads, head_dim),
        jnp.transpose(denominator, (2, 0, 1)).reshape(row_count, query_heads),
    )


def on_device(
    residual,
    norm_gain,
    query_weight,
    key_weight,
    value_weight,
    out_weight,
    post_gain,
    encoder_weight,
    encoder_bias,
    decoder_weight,
    decoder_bias,
):
    token_count = residual.shape[0]
    model_width = decoder_weight.shape[1]
    head_dim = HEAD_DIM
    query_width = query_weight.shape[1]
    key_width = key_weight.shape[1]
    residual_float = residual.astype(jnp.float32)
    scaled = (residual_float * norm_gain).astype(jnp.bfloat16)
    stacked = jnp.concatenate([query_weight, key_weight, value_weight], axis=1)
    projected_part = jnp.dot(scaled, stacked, preferred_element_type=jnp.float32)
    partial_squares = jnp.sum(residual_float * residual_float, axis=1)
    summed, square_sum = lax.psum((projected_part, partial_squares), "dp")
    positions = jnp.arange(token_count)
    queries, keys, values = project(
        summed, square_sum, positions, model_width, query_width, key_width, head_dim
    )
    numerator, denominator = partial_attention(queries, keys, values, positions, positions)
    attended = (
        (numerator / denominator[:, :, None]).astype(jnp.bfloat16).reshape(token_count, query_width)
    )
    heads_part = jnp.dot(attended, out_weight, preferred_element_type=jnp.float32)
    head_out = lax.psum(heads_part, "mp")
    out_squares = lax.psum(jnp.sum(head_out * head_out, axis=1), "dp")
    normed = head_out * lax.rsqrt(out_squares / model_width + epsilon)[:, None] * post_gain
    hidden_columns = (residual_float + normed).astype(jnp.bfloat16)
    portion = lax.all_gather(hidden_columns, "dp", axis=1, tiled=True)
    preact_sum = jnp.dot(portion, encoder_weight, preferred_element_type=jnp.float32)
    preact_sum, hidden = (preact_sum, portion)
    preact = preact_sum + encoder_bias
    active = smoothing * jax.nn.softplus(preact / smoothing)
    active_low = active.astype(jnp.bfloat16)
    gate_slope = jax.nn.sigmoid(preact / smoothing)
    decoder_norms = jnp.sqrt(
        jnp.sum(jnp.square(decoder_weight.astype(jnp.float32)), axis=1) + epsilon
    )
    activity = jnp.sum(active, axis=0)
    rebuilt_part = jnp.dot(active_low, decoder_weight, preferred_element_type=jnp.float32)
    rebuilt = lax.psum(rebuilt_part, ("dp", "mp"))
    error_low = (rebuilt + decoder_bias - hidden.astype(jnp.float32)).astype(jnp.bfloat16)
    feedback = lax.dot_general(
        error_low, decoder_weight, (((1,), (1,)), ((), ())), preferred_element_type=jnp.float32
    )
    outer_sum = lax.dot_general(
        active_low, error_low, (((0,), (0,)), ((), ())), preferred_element_type=jnp.float32
    )
    grad_active = loss_weight * (2.0 * feedback + penalty * decoder_norms)
    grad_preact = grad_active * gate_slope
    encoder_grad = lax.dot_general(
        hidden,
        grad_preact.astype(jnp.bfloat16),
        (((0,), (0,)), ((), ())),
        preferred_element_type=jnp.float32,
    ).astype(jnp.bfloat16)
    encoder_bias_grad = jnp.sum(grad_preact, axis=0)
    decoder_grad = (
        loss_weight
        * (
            2.0 * outer_sum
            + penalty * (activity / decoder_norms)[:, None] * decoder_weight.astype(jnp.float32)
        )
    ).astype(jnp.bfloat16)
    return (encoder_grad, encoder_bias_grad, decoder_grad)


def solution(mesh):
    placed = (
        P(None, "dp"),
        P("dp"),
        P("dp", "mp"),
        P("dp", "mp"),
        P("dp", "mp"),
        P("mp", "dp"),
        P("dp"),
        P(None, ("dp", "mp")),
        P(("dp", "mp")),
        P(("dp", "mp"), None),
        P(),
    )
    return jax.shard_map(
        on_device,
        mesh=mesh,
        in_specs=placed,
        out_specs=(P(None, ("dp", "mp")), P(("dp", "mp")), P(("dp", "mp"), None)),
        check_vma=False,
    )
```

profile of v0, /device:TPU:0, one launch (start us, length us, event | category | flops | bytes accessed | tf_op | source)
XLA Modules:
  0.0 448.3 jit_solution(4388165543059884381)
XLA Ops:
  7.2 0.0 copy-start
  7.2 0.0 all-reduce.4.cloned.1.call-start
  7.2 3.6 fusion.4
  10.9 0.0 all-reduce.4.cloned.1.call-update
  10.9 0.0 all-reduce.6.cloned.1.call-start
  10.9 0.1 fusion.21
  11.0 44.4 %psum.36 = f32[256]{0:T(256)S(1)} all-reduce(f32[256]{0:T(256)S(1)} %fusion.21), channel_id=1, replica_groups=mesh['dp'=16,'mp'=2] {'dp'}, use_global_device_ids=true, to_apply=%region_2.0 | all-reduce | flops 256 | bytes 2048 | tf_op jit(solution)/shard_map/psum | solution.py:90
  55.4 0.7 iota_compare_fusion
  56.1 1.3 multiply_cosine_fusion
  57.4 85.9 %all-reduce.4.cloned.1.call-done = f32[256,2048]{1,0:T(8,128)} async-done(((f32[256,2048]{1,0:T(8,128)}), f32[256,2048]{1,0:T(8,128)}) %all-reduce.4.cloned.1.call-update) | async-done | bytes 2097168 | tf_op jit(solution)/shard_map/psum | solution.py:90
  143.2 1.8 broadcast_multiply_fusion
  145.1 1.0 slice_bitcast_fusion
  146.1 0.8 slice.42
  146.9 0.2 reshape.99
  147.1 1.1 fusion.36
  148.2 0.1 copy-done.4
  148.3 0.2 copy.28
  148.5 0.5 subtract_convert_fusion.1
  149.0 0.9 copy.16
  149.9 0.9 copy.17
  150.8 1.8 copy.25
  152.6 1.1 subtract_convert_fusion.2
  153.7 3.3 fusion.37
  157.0 1.6 fusion.15
  158.6 0.0 copy-start.12
  158.6 0.0 copy-start.13
  158.6 0.1 fusion.14
  158.7 1.0 fusion.39
  159.8 0.0 all-reduce.6.cloned.1.call-update
  159.8 0.0 all-gather.2.cloned.1.call-start
  159.8 17.8 %all-reduce.6.cloned.1.call-done = f32[256,288]{0,1:T(8,128)} async-done(((f32[256,288]{0,1:T(8,128)}), f32[256,288]{0,1:T(8,128)}) %all-reduce.6.cloned.1.call-update) | async-done | bytes 294928 | tf_op jit(solution)/shard_map/psum | solution.py:100
  177.6 1.0 multiply_reduce_fusion
  178.6 42.0 %psum.38 = f32[256]{0:T(256)S(1)} all-reduce(f32[256]{0:T(256)S(1)} %multiply_reduce_fusion), channel_id=1, replica_groups=mesh['dp'=16,'mp'=2] {'dp'}, use_global_device_ids=true, to_apply=%region_6.7 | all-reduce | flops 256 | bytes 2048 | tf_op jit(solution)/shard_map/psum | solution.py:101
  220.6 1.7 fusion.22
  222.3 0.0 all-gather.2.cloned.1.call-update
  222.4 0.2 all-reduce.8.cloned.1.call-start
  222.6 58.1 %all-gather.2.cloned.1.call-done = bf16[256,4608]{0,1:T(8,128)(2,1)} async-done(((bf16[256,288]{0,1:T(8,128)(2,1)}), bf16[256,4608]{0,1:T(8,128)(2,1)}) %all-gather.2.cloned.1.call-update) | async-done | bytes 2359312 | tf_op jit(solution)/shard_map/all_gather | solution.py:104
  280.7 2.8 fusion.29
  283.5 3.3 fusion.34
  286.8 0.0 all-reduce.8.cloned.1.call-update
  286.8 0.0 copy-start.11
  286.8 2.2 fusion.3
  289.0 141.6 %all-reduce.8.cloned.1.call-done = f32[256,4608]{0,1:T(8,128)} async-done(((f32[256,4608]{0,1:T(8,128)}), f32[256,4608]{0,1:T(8,128)}) %all-reduce.8.cloned.1.call-update) | async-done | bytes 4718608 | tf_op jit(solution)/shard_map/psum | solution.py:116
  430.6 4.2 subtract_convert_fusion
  434.9 3.1 fusion.2
  438.0 1.4 fusion.38
  439.4 0.3 copy-done.1
  439.6 2.2 convolution_convert_fusion
  (29 shorter events, 0.1 us)
Async XLA Ops:
  7.2 273.5 %copy-start = (bf16[4608,256]{1,0:T(8,128)(2,1)S(1)}, bf16[4608,256]{1,0:T(8,128)(2,1)}, u32[]{:S(2)}) copy-start(bf16[4608,256]{1,0:T(8,128)(2,1)} %param.18) | copy-start | bytes 7077892
  7.2 3.8 copy-start.6
  7.2 136.0 %all-reduce.4.cloned.1.call-start = ((), (), s32[]{:S(2)}) async-start(), calls=%async_computation | async-start | bytes 4194304 | tf_op jit(solution)/shard_map/psum | solution.py:90
  10.9 166.7 %all-reduce.6.cloned.1.call-start = ((), (), s32[]{:S(2)}) async-start(), calls=%async_computation.1 | async-start | bytes 589824 | tf_op jit(solution)/shard_map/psum | solution.py:100
  147.1 1.2 copy-start.4
  147.1 1.4 copy-start.7
  147.1 1.4 copy-start.8
  148.5 4.1 copy-start.5
  153.7 3.3 copy-start.9
  157.0 1.7 copy-start.10
  158.6 62.0 %copy-start.12 = (f32[288]{0:T(512)S(1)}, f32[288]{0:T(512)}, u32[]{:S(2)}) copy-start(f32[288]{0:T(512)} %param.17) | copy-start | bytes 3460
  158.6 122.1 %copy-start.13 = (f32[256]{0:T(256)S(1)}, f32[256]{0:T(256)}, u32[]{:S(2)}) copy-start(f32[256]{0:T(256)} %param.19) | copy-start | bytes 3076
  159.8 120.9 %all-gather.2.cloned.1.call-start = ((), (), s32[]{:S(2)}) async-start(), calls=%async_computation.2 | async-start | bytes 2506752 | tf_op jit(solution)/shard_map/all_gather | solution.py:104
  222.4 208.3 %all-reduce.8.cloned.1.call-start = ((), (), s32[]{:S(2)}) async-start(), calls=%async_computation.3 | async-start | bytes 9437184 | tf_op jit(solution)/shard_map/psum | solution.py:116
  280.7 2.8 copy-start.2
  286.8 143.8 %copy-start.11 = (f32[4608]{0:T(1024)S(1)}, f32[4608]{0:T(1024)}, u32[]{:S(2)}) copy-start(f32[4608]{0:T(1024)} %param.21) | copy-start | bytes 55300
  430.6 4.3 copy-start.3
  438.0 1.7 copy-start.1
Sparse Core Ops, SparseCore 0:
  14.1 129.1 all-reduce.3
  159.9 17.6 all-reduce.5
  222.5 58.1 all-gather.1
  287.1 143.4 all-reduce.7
where the time goes:
time: 449 us; the launch traced here: 448 us
  waiting for transfers between devices  303 us (67%)
  blocking collectives  86.3 us (19%)
  matrix products  22.3 us (5%)
  other arithmetic  14.7 us (3%)
  between operations  14 us (3%)
  local copies, waits for them, and re-layouts  7.29 us (2%)
    psum x1, waiting for transfers between devices, on_device(): rebuilt = lax.psum(rebuilt_part, ('dp', 'mp'))  142 us
    psum x1, waiting for transfers between devices, on_device(): summed, square_sum = lax.psum((projected_part, partial_squares), 'dp')  85.9 us
    all_gather x1, waiting for transfers between devices, on_device(): portion = lax.all_gather(hidden_columns, 'dp', axis=1, tiled=True)  58.1 us
    psum x1, blocking collectives, on_device(): summed, square_sum = lax.psum((projected_part, partial_squares), 'dp')  44.4 us
    psum x1, blocking collectives, on_device(): out_squares = lax.psum(jnp.sum(head_out * head_out, axis=1), 'dp')  42 us
    psum x1, waiting for transfers between devices, on_device(): head_out = lax.psum(heads_part, 'mp')  17.8 us
  transfers between devices with their start and end apart: 4, of which 4 were waited for; matrix products, arithmetic and copies ran while one was open for 1% of the time, Pallas kernels for 0%

commit v1 on v0

--- a/solution.py
+++ b/solution.py
@@ -113,7 +113,7 @@
     )
     activity = jnp.sum(active, axis=0)
     rebuilt_part = jnp.dot(active_low, decoder_weight, preferred_element_type=jnp.float32)
-    rebuilt = lax.psum(rebuilt_part, ("dp", "mp"))
+    rebuilt = lax.psum(lax.psum(rebuilt_part, axis_name="mp"), "dp")
     error_low = (rebuilt + decoder_bias - hidden.astype(jnp.float32)).astype(jnp.bfloat16)
     feedback = lax.dot_general(
         error_low, decoder_weight, (((1,), (1,)), ((), ())), preferred_element_type=jnp.float32

time: 449 us -> 520 us (1.16)
  waiting for transfers between devices: 303 us -> 374 us
    psum x1 -> x2, waiting for transfers between devices: 142 us -> 212 us  [on_device(): rebuilt = lax.psum(lax.psum(rebuilt_part, axis_name='mp'), 'dp')]
  transfers between devices with their start and end apart: 4 -> 5, of which waited for: 4 -> 5; matrix products, arithmetic and copies ran while one was open for 1% -> 1% of each run, Pallas kernels for 0% -> 0%
where the time goes in v1:
time: 520 us; the launch traced here: 519 us
  waiting for transfers between devices  374 us (72%)
  blocking collectives  86.3 us (17%)
  matrix products  22.3 us (4%)
  other arithmetic  14.7 us (3%)
  between operations  14 us (3%)
  local copies, waits for them, and re-layouts  7.29 us (1%)
    psum x2, waiting for transfers between devices, on_device(): rebuilt = lax.psum(lax.psum(rebuilt_part, axis_name='mp'), 'dp')  212 us
    psum x1, waiting for transfers between devices, on_device(): summed, square_sum = lax.psum((projected_part, partial_squares), 'dp')  85.9 us
    all_gather x1, waiting for transfers between devices, on_device(): portion = lax.all_gather(hidden_columns, 'dp', axis=1, tiled=True)  58.3 us
    psum x1, blocking collectives, on_device(): summed, square_sum = lax.psum((projected_part, partial_squares), 'dp')  44.4 us
    psum x1, blocking collectives, on_device(): out_squares = lax.psum(jnp.sum(head_out * head_out, axis=1), 'dp')  42 us
    psum x1, waiting for transfers between devices, on_device(): head_out = lax.psum(heads_part, 'mp')  17.8 us
  transfers between devices with their start and end apart: 5, of which 5 were waited for; matrix products, arithmetic and copies ran while one was open for 1% of the time, Pallas kernels for 0%

profile of v1, /device:TPU:0, one launch (start us, length us, event | category | flops | bytes accessed | tf_op | source)
XLA Modules:
  0.0 519.2 jit_solution(12731090498127655229)
XLA Ops:
  7.2 0.0 copy-start
  7.2 0.0 all-reduce.5.cloned.1.call-start
  7.2 3.6 fusion.4
  10.9 0.0 all-reduce.5.cloned.1.call-update
  10.9 0.0 all-reduce.7.cloned.1.call-start
  10.9 0.1 fusion.21
  11.0 44.4 %psum.43 = f32[256]{0:T(256)S(1)} all-reduce(f32[256]{0:T(256)S(1)} %fusion.21), channel_id=1, replica_groups=mesh['dp'=16,'mp'=2] {'dp'}, use_global_device_ids=true, to_apply=%region_2.0 | all-reduce | flops 256 | bytes 2048 | tf_op jit(solution)/shard_map/psum | solution.py:90
  55.4 0.7 iota_compare_fusion
  56.1 1.3 multiply_cosine_fusion
  57.4 85.9 %all-reduce.5.cloned.1.call-done = f32[256,2048]{1,0:T(8,128)} async-done(((f32[256,2048]{1,0:T(8,128)}), f32[256,2048]{1,0:T(8,128)}) %all-reduce.5.cloned.1.call-update) | async-done | bytes 2097168 | tf_op jit(solution)/shard_map/psum | solution.py:90
  143.2 1.8 broadcast_multiply_fusion
  145.1 1.0 slice_bitcast_fusion
  146.1 0.8 slice.42
  146.9 0.2 reshape.99
  147.1 1.1 fusion.36
  148.2 0.1 copy-done.4
  148.3 0.2 copy.28
  148.5 0.5 subtract_convert_fusion.1
  149.0 0.9 copy.16
  149.9 0.9 copy.17
  150.8 1.8 copy.25
  152.6 1.1 subtract_convert_fusion.2
  153.7 3.3 fusion.37
  157.0 1.6 fusion.15
  158.6 0.1 fusion.14
  158.7 1.0 fusion.39
  159.8 0.0 all-reduce.7.cloned.1.call-update
  159.8 0.0 all-gather.2.cloned.1.call-start
  159.8 17.8 %all-reduce.7.cloned.1.call-done = f32[256,288]{0,1:T(8,128)} async-done(((f32[256,288]{0,1:T(8,128)}), f32[256,288]{0,1:T(8,128)}) %all-reduce.7.cloned.1.call-update) | async-done | bytes 294928 | tf_op jit(solution)/shard_map/psum | solution.py:100
  177.6 1.0 multiply_reduce_fusion
  178.6 42.0 %psum.45 = f32[256]{0:T(256)S(1)} all-reduce(f32[256]{0:T(256)S(1)} %multiply_reduce_fusion), channel_id=1, replica_groups=mesh['dp'=16,'mp'=2] {'dp'}, use_global_device_ids=true, to_apply=%region_6.7 | all-reduce | flops 256 | bytes 2048 | tf_op jit(solution)/shard_map/psum | solution.py:101
  220.6 1.7 fusion.22
  222.3 0.0 all-gather.2.cloned.1.call-update
  222.4 0.0 all-reduce.9.cloned.1.call-start
  222.4 58.3 %all-gather.2.cloned.1.call-done = bf16[256,4608]{0,1:T(8,128)(2,1)} async-done(((bf16[256,288]{0,1:T(8,128)(2,1)}), bf16[256,4608]{0,1:T(8,128)(2,1)}) %all-gather.2.cloned.1.call-update) | async-done | bytes 2359312 | tf_op jit(solution)/shard_map/all_gather | solution.py:104
  280.7 2.8 fusion.29
  283.5 3.3 fusion.34
  286.8 0.0 all-reduce.9.cloned.1.call-update
  286.8 0.2 all-reduce.11.cloned.1.call-start
  287.0 27.9 %all-reduce.9.cloned.1.call-done = f32[256,4608]{0,1:T(8,128)} async-done(((f32[256,4608]{0,1:T(8,128)}), f32[256,4608]{0,1:T(8,128)}) %all-reduce.9.cloned.1.call-update) | async-done | bytes 4718608 | tf_op jit(solution)/shard_map/psum | solution.py:116
  314.9 0.0 all-reduce.11.cloned.1.call-update
  314.9 2.2 fusion.3
  317.2 184.3 %all-reduce.11.cloned.1.call-done = f32[256,4608]{0,1:T(8,128)} async-done(((f32[256,4608]{0,1:T(8,128)}), f32[256,4608]{0,1:T(8,128)}) %all-reduce.11.cloned.1.call-update) | async-done | bytes 4718608 | tf_op jit(solution)/shard_map/psum | solution.py:116
  501.4 4.2 subtract_convert_fusion
  505.7 3.1 fusion.2
  508.8 1.4 fusion.38
  510.2 0.3 copy-done.1
  510.4 2.2 convolution_convert_fusion
  (32 shorter events, 0.1 us)
Async XLA Ops:
  7.2 273.5 %copy-start = (bf16[4608,256]{1,0:T(8,128)(2,1)S(1)}, bf16[4608,256]{1,0:T(8,128)(2,1)}, u32[]{:S(2)}) copy-start(bf16[4608,256]{1,0:T(8,128)(2,1)} %param.18) | copy-start | bytes 7077892
  7.2 3.8 copy-start.6
  7.2 136.0 %all-reduce.5.cloned.1.call-start = ((), (), s32[]{:S(2)}) async-start(), calls=%async_computation | async-start | bytes 4194304 | tf_op jit(solution)/shard_map/psum | solution.py:90
  10.9 166.7 %all-reduce.7.cloned.1.call-start = ((), (), s32[]{:S(2)}) async-start(), calls=%async_computation.1 | async-start | bytes 589824 | tf_op jit(solution)/shard_map/psum | solution.py:100
  147.1 1.2 copy-start.4
  147.1 1.4 copy-start.7
  147.1 1.4 copy-start.8
  148.5 4.1 copy-start.5
  153.7 3.3 copy-start.9
  157.0 1.7 copy-start.10
  158.6 62.0 %copy-start.12 = (f32[288]{0:T(512)S(1)}, f32[288]{0:T(512)}, u32[]{:S(2)}) copy-start(f32[288]{0:T(512)} %param.17) | copy-start | bytes 3460
  158.6 122.1 %copy-start.13 = (f32[256]{0:T(256)S(1)}, f32[256]{0:T(256)}, u32[]{:S(2)}) copy-start(f32[256]{0:T(256)} %param.19) | copy-start | bytes 3076
  159.8 120.9 %all-gather.2.cloned.1.call-start = ((), (), s32[]{:S(2)}) async-start(), calls=%async_computation.2 | async-start | bytes 2506752 | tf_op jit(solution)/shard_map/all_gather | solution.py:104
  222.4 92.5 %all-reduce.9.cloned.1.call-start = ((), (), s32[]{:S(2)}) async-start(), calls=%async_computation.3 | async-start | bytes 9437184 | tf_op jit(solution)/shard_map/psum | solution.py:116
  280.7 2.8 copy-start.2
  286.8 214.6 %all-reduce.11.cloned.1.call-start = ((), (), s32[]{:S(2)}) async-start(), calls=%async_computation.4 | async-start | bytes 9437184 | tf_op jit(solution)/shard_map/psum | solution.py:116
  314.9 186.5 %copy-start.11 = (f32[4608]{0:T(1024)S(1)}, f32[4608]{0:T(1024)}, u32[]{:S(2)}) copy-start(f32[4608]{0:T(1024)} %param.21) | copy-start | bytes 55300
  501.4 4.3 copy-start.3
  508.8 1.7 copy-start.1
Sparse Core Ops, SparseCore 0:
  14.1 129.1 all-reduce.4
  159.9 17.6 all-reduce.6
  222.5 58.1 all-gather.1
  286.9 27.9 all-reduce.8
  320.5 180.9 all-reduce.10
